TPU v7x, 256 devices: a whole 4x4x8 slice. The times are simulated.
256 devices in a mesh: star: 64 (over y, z_lo, x, core), gas: 4 (over z_hi).
Axes of the slice: x: 4, y: 4, z: 8 (z_hi: 4, z_lo: 2; z = z_hi * 2 + z_lo), core: 2. Of those that a mesh axis runs over, the one named last changes fastest.
Arguments:
- star_pos: float32 [3, 131072], P(None, ('star', 'gas')), may hold values from 0 to 32
- star_vel: float32 [3, 131072], P(None, ('star', 'gas')), may hold values from -6 to 6
- star_accel: float32 [6, 131072], P(None, ('star', 'gas')), may hold values from -6 to 6
- star_mass: float32 [131072], P(('star', 'gas')), may hold values from 0.1 to 2
- active: int32 [2048], replicated, may hold values from 0 to 131071, as said below
- density: float32 [256, 32, 64], P('star', 'gas'), may hold values from 0.5 to 4
- flow_in: float32 [3, 256, 32, 64], P(None, 'star', 'gas'), may hold values from -2 to 2
- field_in: float32 [3, 256, 32, 64], P(None, 'star', 'gas'), may hold values from -4 to 4
Outputs:
- star_new: float32 [12, 131072], P(None, ('star', 'gas'))
- flow: float32 [3, 256, 32, 64], P(None, 'star', 'gas')
- field_out: float32 [3, 256, 32, 64], P(None, 'star', 'gas')
Inputs may be any that keep to these rules, and one draw needn't show every extreme that they name: Distinct and increasing; among the 512 consecutive indices of one device at most 24 are active, and in every draw some device holds exactly 24.
All inputs are finite; a program needn't handle non-finite values.
Results may differ from a plain program's by a relative error of at most 0.0001.
Values sent between devices are 32-bit elements; how exact they have to be, the bound alone decides.
A program may use at most 64 MiB of HBM per device.

v0:
```python
import math
import jax
import jax.numpy as jnp
from jax import lax
from jax.sharding import PartitionSpec as P

MOST = 24
gravity = 0.02
soften = 4.0
time_step = 1.5
field_step = 0.1
highest = lax.Precision.HIGHEST


def with_halo(block, sides, width):
    for axis, dim in sides:
        count = lax.axis_size(axis)
        forward = [(i, i + 1) for i in range(count - 1)]
        forward.append((count - 1, 0))
        backward = [(target, source) for source, target in forward]
        low = lax.ppermute(
            lax.slice_in_dim(block, block.shape[dim] - width, None, axis=dim), axis, forward
        )
        high = lax.ppermute(lax.slice_in_dim(block, 0, width, axis=dim), axis, backward)
        block = jnp.concatenate([low, block, high], axis=dim)
    return block


def grad_x(values):
    return 0.5 * (values[2:, 1:-1] - values[:-2, 1:-1])


def grad_y(values):
    return 0.5 * (values[1:-1, 2:] - values[1:-1, :-2])


def grad_z(values):
    return 0.5 * (jnp.roll(values, -1, 2) - jnp.roll(values, 1, 2))[1:-1, 1:-1]


def trim_rim(values):
    return values[1:-1, 1:-1]


def curl_of(comp_a, comp_b, comp_c):
    return (
        grad_y(comp_c) - grad_z(comp_b),
        grad_z(comp_a) - grad_x(comp_c),
        grad_x(comp_b) - grad_y(comp_a),
    )


def cross_of(lhs_vec, rhs_vec):
    return (
        lhs_vec[1] * rhs_vec[2] - lhs_vec[2] * rhs_vec[1],
        lhs_vec[2] * rhs_vec[0] - lhs_vec[0] * rhs_vec[2],
        lhs_vec[0] * rhs_vec[1] - lhs_vec[1] * rhs_vec[0],
    )


def field_rate(padded_field, padded_flow, padded_density):
    current = curl_of(padded_field[0], padded_field[1], padded_field[2])
    inner_field = (trim_rim(padded_field[0]), trim_rim(padded_field[1]), trim_rim(padded_field[2]))
    inner_flow = (trim_rim(padded_flow[0]), trim_rim(padded_flow[1]), trim_rim(padded_flow[2]))
    resist = trim_rim(padded_density) ** (-1.5)
    lorentz = cross_of(current, inner_field)
    drift = cross_of(lorentz, inner_field)
    motion = cross_of(inner_flow, inner_field)
    emf_a = motion[0] + resist * drift[0]
    emf_b = motion[1] + resist * drift[1]
    emf_c = motion[2] + resist * drift[2]
    return jnp.stack(curl_of(emf_a, emf_b, emf_c))


def pair_terms(target, resident, cell_place, cell_mass):
    star_gap = resident[0:3, None, :] - target[0:3, :, None]
    rel_vel = resident[3:6, None, :] - target[3:6, :, None]
    inv_r = lax.rsqrt(jnp.sum(star_gap * star_gap, 0) + soften)
    weight = gravity * resident[6][None, :] * inv_r * inv_r * inv_r
    star_acc = jnp.sum(weight[None] * star_gap, 2)
    approach = jnp.sum(star_gap * rel_vel, 0)
    star_jerk = jnp.sum(
        weight[None] * (rel_vel - 3.0 * (approach * inv_r * inv_r)[None] * star_gap), 2
    )
    cell_gap = cell_place[:, None, :] - target[0:3, :, None]
    inv_g = lax.rsqrt(jnp.sum(cell_gap * cell_gap, 0) + soften)
    inv_cube = gravity * inv_g * inv_g * inv_g
    gas_acc = jnp.sum((inv_cube * cell_mass[None, :])[None] * cell_gap, 2)
    cell_kick = -jnp.sum((inv_cube * target[6][:, None])[None] * cell_gap, 1)
    return (jnp.concatenate([star_acc + gas_acc, star_jerk], 0), cell_kick)


def all_terms(targets, resident, cell_place, cell_mass):
    target_total = targets.shape[1]
    block_width = math.gcd(target_total, 64)
    blocks = targets.reshape(7, target_total // block_width, block_width).transpose(1, 0, 2)

    def one_block(running, target_block):
        terms_here, cell_kick = pair_terms(target_block, resident, cell_place, cell_mass)
        return (running + cell_kick, terms_here)

    kick_sum, block_terms = lax.scan(one_block, jnp.zeros(cell_place.shape, jnp.float32), blocks)
    return (block_terms.transpose(1, 0, 2).reshape(6, target_total), kick_sum)


def body(star_pos, star_vel, star_accel, star_mass, active, density, flow_in, field_in):
    resident_total = star_pos.shape[1]
    old_acc = star_accel[0:3]
    old_jerk = star_accel[3:6]
    pred_pos = (
        star_pos
        + time_step * star_vel
        + time_step**2 / 2.0 * old_acc
        + time_step**3 / 6.0 * old_jerk
    )
    pred_vel = star_vel + time_step * old_acc + time_step**2 / 2.0 * old_jerk
    resident = jnp.concatenate([pred_pos, pred_vel, star_mass[None]], 0)
    my_rank = lax.axis_index("star") * lax.axis_size("gas") + lax.axis_index("gas")
    owner_of = active // resident_total
    local_slot = active % resident_total
    is_mine = owner_of == my_rank
    rows_iota = jnp.arange(resident_total, dtype=jnp.int32)
    owned = (is_mine[None, :] & (local_slot[None, :] == rows_iota[:, None])).astype(jnp.float32)
    active_mask = jnp.sum(owned, 1) > 0.5
    ext_x, ext_y, ext_z = density.shape
    grid_shape = (ext_x, ext_y, ext_z)
    coord_x = (lax.axis_index("star") * ext_x + jnp.arange(ext_x)).astype(jnp.float32) + 0.5
    coord_y = (lax.axis_index("gas") * ext_y + jnp.arange(ext_y)).astype(jnp.float32) + 0.5
    coord_z = jnp.arange(ext_z).astype(jnp.float32) + 0.5
    cell_place = jnp.stack(
        [
            jnp.broadcast_to(coord_x[:, None, None], grid_shape),
            jnp.broadcast_to(coord_y[None, :, None], grid_shape),
            jnp.broadcast_to(coord_z[None, None, :], grid_shape),
        ]
    ).reshape(3, -1)
    cell_mass = density.reshape(-1)
    order_rank = jnp.cumsum(is_mine.astype(jnp.int32)) - 1
    slot_iota = jnp.arange(MOST, dtype=jnp.int32)
    slot_pick = (is_mine[:, None] & (order_rank[:, None] == slot_iota[None, :])).astype(jnp.float32)
    selector = jnp.dot(owned, slot_pick, precision=highest)
    packed = jnp.dot(resident, selector, precision=highest)
    targets = lax.all_gather(packed, ("star", "gas"), axis=1, tiled=True)
    partial_terms, kick_sum = all_terms(targets, resident, cell_place, cell_mass)
    summed = lax.psum(partial_terms, ("star", "gas"))
    mine_terms = lax.dynamic_slice_in_dim(summed, my_rank * MOST, MOST, 1)
    own_terms = jnp.dot(mine_terms, selector.T, precision=highest)
    new_acc = own_terms[0:3]
    new_jerk = own_terms[3:6]
    vel_one = (
        star_vel
        + time_step * (old_acc + new_acc) / 2.0
        + time_step**2 * (old_jerk - new_jerk) / 12.0
    )
    pos_one = (
        star_pos
        + time_step * (star_vel + vel_one) / 2.0
        + time_step**2 * (old_acc - new_acc) / 12.0
    )
    updated = jnp.concatenate([pos_one, vel_one, new_acc, new_jerk], 0)
    base = jnp.concatenate([star_pos, star_vel, star_accel], 0)
    star_new = jnp.where(active_mask[None, :], updated, base)
    flow = flow_in + time_step * kick_sum.reshape(3, ext_x, ext_y, ext_z)

    def rate_of(values):
        padded = with_halo(
            jnp.concatenate([values, flow, density[None]], 0), (("star", 1), ("gas", 2)), 2
        )
        return field_rate(padded[0:3], padded[3:6], padded[6])

    first_section = field_in + field_step * rate_of(field_in)
    field_out = 0.5 * (field_in + first_section + field_step * rate_of(first_section))
    return (star_new, flow, field_out)


def solution(mesh):
    placed = (
        P(None, ("star", "gas")),
        P(None, ("star", "gas")),
        P(None, ("star", "gas")),
        P(("star", "gas")),
        P(),
        P("star", "gas", None),
        P(None, "star", "gas", None),
        P(None, "star", "gas", None),
    )
    return jax.shard_map(
        body,
        mesh=mesh,
        in_specs=placed,
        out_specs=(
            P(None, ("star", "gas")),
            P(None, "star", "gas", None),
            P(None, "star", "gas", None),
        ),
        check_vma=False,
    )
```

profile of v0, /device:TPU:1, one launch (start us, length us, event | category | flops | bytes accessed | tf_op | source)
XLA Modules:
  0.0 1057.4 jit_solution(8387592304197424626)
XLA Ops:
  7.3 0.7 add_select_fusion
  8.0 0.7 convert_bitcast_fusion
  9.3 1.4 fusion.14
  10.9 629.3 %all-gather = f32[256,24,7]{1,2,0:T(8,128)S(1)} all-gather(f32[1,24,7]{1,2,0:T(8,128)S(1)} %convolution_bitcast_fusion), channel_id=1, replica_groups=mesh['star'=64,'gas'=4] {'star','gas'}, dimensions={0}, use_global_device_ids=true | all-gather | bytes 172704 | tf_op jit(solution)/shard_map/all_gather | solution.py:143
  640.4 0.5 reshape.159
  641.8 144.5 %while.14 = (s32[]{:T(128)}, f32[3,2048]{1,0:T(4,128)S(1)}, f32[96,6,64]{2,1,0:T(8,128)S(1)}, f32[3,4,8,64]{3,2,1,0:T(8,128)}, f32[96,7,64]{2,0,1:T(8,128)S(1)},...) while((s32[]{:T(128)}, f32[3,2048]{1,0:T(4,128)S(1)}, ...), condition=%wide.wide.region_11.12_spmd.clone, body=%wide.wide.region_3.11_spmd.clone.sunk | while | flops 5353989 | bytes 4405187 | solution.py:102
  642.8 0.5 fusion.148
  644.3 0.5 fusion.148
  645.8 0.5 fusion.148
  647.3 0.5 fusion.148
  786.5 0.7 pad_maximum_fusion.9
  787.4 6.9 collective-permute-start.1
  794.3 0.8 reshape.156
  795.1 0.8 convert_reduce_fusion
  796.1 3.6 collective-permute-start.3
  799.7 1.9 collective-permute-done.2
  802.8 7.0 collective-permute-start.5
  809.8 231.5 %all-reduce.2.cloned.1.call-done = f32[6,6144]{1,0:T(8,128)} async-done(((f32[6,6144]{1,0:T(8,128)}), f32[6,6144]{1,0:T(8,128)}) %all-reduce.2.cloned.1.call-update) | async-done | bytes 147472 | tf_op jit(solution)/shard_map/psum | solution.py:145
  1041.2 0.9 fusion.97
  1042.2 0.9 collective-permute-start.6
  1043.1 2.7 collective-permute-start.7
  1045.9 0.6 maximum_select_fusion
  1046.5 2.1 collective-permute-done.6
  1049.9 0.6 fusion.58
  (1337 shorter events, 139.1 us)
Async XLA Ops:
  7.2 1034.1 %all-reduce.2.cloned.1.call-start = ((), (), s32[]{:S(2)}) async-start(), calls=%async_computation | async-start | bytes 393216 | tf_op jit(solution)/shard_map/psum | solution.py:145
  9.3 1.4 copy-start.5
  9.3 1.4 copy-start.7
  9.3 1.4 copy-start.8
  9.3 1.5 copy-start.6
  640.3 1.0 copy-start.2
  641.2 0.6 copy-start.4
  641.8 144.7 %copy-start.9 = (f32[3,4,8,64]{3,2,1,0:T(8,128)S(1)}, f32[3,4,8,64]{3,2,1,0:T(8,128)}, u32[]{:S(2)}) copy-start(f32[3,4,8,64]{3,2,1,0:T(8,128)} %param.16) | copy-start | bytes 73732
  641.8 144.7 %copy-start.1 = (f32[3,4,8,64]{3,2,1,0:T(8,128)S(1)}, f32[3,4,8,64]{3,2,1,0:T(8,128)}, u32[]{:S(2)}) copy-start(f32[3,4,8,64]{3,2,1,0:T(8,128)} %param.17) | copy-start | bytes 73732
  786.4 9.5 copy-start.3
  786.5 262.1 %copy-start = (f32[3,4,8,64]{3,2,1,0:T(8,128)}, f32[3,4,8,64]{3,2,1,0:T(8,128)S(1)}, u32[]{:S(2)}) copy-start(f32[3,4,8,64]{3,2,1,0:T(8,128)S(1)} %add.174) | copy-start | bytes 73732
  787.3 8.6 collective-permute-start
  787.4 8.5 collective-permute-start.1
  796.0 5.5 collective-permute-start.2
  796.1 5.4 collective-permute-start.3
  802.7 239.5 %collective-permute-start.4 = (f32[7,2,8,64]{3,2,1,0:T(8,128)S(1)}, f32[7,2,8,64]{3,2,1,0:T(8,128)S(1)}, u32[]{:S(2)}, u32[]{:S(2)}) collective-permute-start(f32[7,2,8,64]{3,2,1,0:T(8,128)S(1)} %get-tuple-element.178), channel_id=1, source_target_pairs={{0,4},{4,8},{8,12},{12,16},{16,20},{20,24},{24,28},{28,32},{32,36}... | collective-permute-start | bytes 86024 | tf_op jit(solution)/shard_map/ppermute | solution.py:21
  802.8 239.4 %collective-permute-start.5 = (f32[7,2,8,64]{3,2,1,0:T(8,128)S(1)}, f32[7,2,8,64]{3,2,1,0:T(8,128)S(1)}, u32[]{:S(2)}, u32[]{:S(2)}) collective-permute-start(f32[7,2,8,64]{3,2,1,0:T(8,128)S(1)} %get-tuple-element.179), channel_id=1, source_target_pairs={{4,0},{8,4},{12,8},{16,12},{20,16},{24,20},{28,24},{32,28},{36,32}... | collective-permute-start | bytes 86024 | tf_op jit(solution)/shard_map/ppermute | solution.py:24
  1042.2 6.4 collective-permute-start.6
  1043.1 5.5 collective-permute-start.7
Sparse Core Ops, SparseCore 0:
  795.3 245.9 all-reduce.1
where the time goes:
time: 1060 us
  blocking collectives  629 us (59%)
  waiting for transfers between devices  235 us (22%)
  other arithmetic  139 us (13%)
  starting transfers between devices  21.4 us (2%)
  between operations  14.4 us (1%)
    all_gather x1, blocking collectives, body(): targets = lax.all_gather(packed, ('star', 'gas'), axis=1, tiled=True)  629 us
    psum x1, waiting for transfers between devices, body(): summed = lax.psum(partial_terms, ('star', 'gas'))  231 us
    reduce_sum x96, other arithmetic, pair_terms(): gas_acc = jnp.sum((inv_cube * cell_mass[None, :])[None] * cell_gap, 2)  48.2 us
    reduce_sum x96, other arithmetic, pair_terms(): star_acc = jnp.sum(weight[None] * star_gap, 2)  27.3 us
  transfers between devices with their start and end apart: 9, of which 3 were waited for; matrix products, arithmetic and copies ran while one was open for 0% of the time, Pallas kernels for 0%

commit v1 on v0

--- a/solution.py
+++ b/solution.py
@@ -142,7 +142,7 @@
     packed = jnp.dot(resident, selector, precision=highest)
     targets = lax.all_gather(packed, ("star", "gas"), axis=1, tiled=True)
     partial_terms, kick_sum = all_terms(targets, resident, cell_place, cell_mass)
-    summed = lax.psum(partial_terms, ("star", "gas"))
+    summed = jnp.sum(lax.all_gather(partial_terms, ("star", "gas")), axis=0)
     mine_terms = lax.dynamic_slice_in_dim(summed, my_rank * MOST, MOST, 1)
     own_terms = jnp.dot(mine_terms, selector.T, precision=highest)
     new_acc = own_terms[0:3]

time: 1060 us -> 1590 us (1.50)
  waiting for transfers between devices: 235 us -> 741 us
  other arithmetic: 139 us -> 157 us
    all_gather x0 -> x1, waiting for transfers between devices: none -> 737 us  [body(): summed = jnp.sum(lax.all_gather(partial_terms, ('star', 'gas')), axis=0)]
    psum x1 -> x0, waiting for transfers between devices: 231 us -> none  [body(): summed = lax.psum(partial_terms, ('star', 'gas'))]
    reduce_sum x0 -> x1, other arithmetic: none -> 17.7 us  [body(): summed = jnp.sum(lax.all_gather(partial_terms, ('star', 'gas')), axis=0)]
  transfers between devices with their start and end apart: 9 -> 9, of which waited for: 3 -> 6; matrix products, arithmetic and copies ran while one was open for 0% -> 0% of each run, Pallas kernels for 0% -> 0%
where the time goes in v1:
time: 1590 us; the launch traced here: 1580 us
  waiting for transfers between devices  741 us (47%)
  blocking collectives  629 us (40%)
  other arithmetic  157 us (10%)
  starting transfers between devices  23.5 us (1%)
    all_gather x1, waiting for transfers between devices, body(): summed = jnp.sum(lax.all_gather(partial_terms, ('star', 'gas')), axis=0)  737 us
    all_gather x1, blocking collectives, body(): targets = lax.all_gather(packed, ('star', 'gas'), axis=1, tiled=True)  629 us
    reduce_sum x96, other arithmetic, pair_terms(): gas_acc = jnp.sum((inv_cube * cell_mass[None, :])[None] * cell_gap, 2)  48.2 us
  transfers between devices with their start and end apart: 9, of which 6 were waited for; matrix products, arithmetic and copies ran while one was open for 0% of the time, Pallas kernels for 0%

profile of v1, /device:TPU:1, one launch (start us, length us, event | category | flops | bytes accessed | tf_op | source)
XLA Modules:
  0.0 1583.9 jit_solution(17852836197925867691)
XLA Ops:
  7.3 0.7 add_select_fusion
  8.0 0.8 mul.753
  8.8 0.7 convert_bitcast_fusion
  10.3 0.8 multiply_add_fusion.8
  11.2 1.4 fusion.14
  12.7 629.3 %all-gather = f32[256,24,7]{1,2,0:T(8,128)S(1)} all-gather(f32[1,24,7]{1,2,0:T(8,128)S(1)} %convolution_bitcast_fusion), channel_id=1, replica_groups=mesh['star'=64,'gas'=4] {'star','gas'}, dimensions={0}, use_global_device_ids=true | all-gather | bytes 172704 | tf_op jit(solution)/shard_map/all_gather | solution.py:143
  642.2 0.5 reshape.155
  642.8 145.6 %while.14 = (s32[]{:T(128)}, f32[3,2048]{1,0:T(4,128)S(1)}, f32[96,6,64]{2,1,0:T(8,128)S(1)}, f32[3,4,8,64]{3,2,1,0:T(8,128)}, f32[96,7,64]{2,0,1:T(8,128)S(1)},...) while((s32[]{:T(128)}, f32[3,2048]{1,0:T(4,128)S(1)}, ...), condition=%wide.wide.region_11.12_spmd.clone, body=%wide.wide.region_3.11_spmd.clone.sunk | while | flops 5353989 | bytes 4405195 | solution.py:102
  643.8 0.5 fusion.148
  645.3 0.5 fusion.148
  646.8 0.5 fusion.148
  788.6 0.8 all_gather_reshape.3
  789.7 6.9 collective-permute-start.1
  796.5 0.6 collective-permute-done
  797.6 3.6 collective-permute-start.3
  801.1 1.6 collective-permute-done.2
  804.0 8.9 collective-permute-start.5
  812.9 0.8 convert_reduce_fusion
  814.0 3.7 collective-permute-start.7
  817.7 2.0 collective-permute-done.6
  821.0 0.6 fusion.58
  821.6 736.9 %all-gather.3.cloned.1.call-done = f32[256,6,6144]{2,1,0:T(8,128)} async-done(((f32[1,6,6144]{2,1,0:T(8,128)}), f32[256,6,6144]{2,1,0:T(8,128)}) %all-gather.3.cloned.1.call-update) | async-done | bytes 37748752 | tf_op jit(solution)/shard_map/all_gather | solution.py:145
  1558.5 17.7 %reduce_sum.82 = f32[6,6144]{1,0:T(8,128)S(1)} reduce(f32[256,6,6144]{2,1,0:T(8,128)} %all-gather.3.cloned.1.call-done, f32[]{:T(128)} %constant.94.clone.1), dimensions={0}, to_apply=%region_12.13 | reduce | flops 9400320 | bytes 37896196 | tf_op jit(solution)/shard_map/reduce_sum | solution.py:145
  1576.4 0.6 maximum_select_fusion
  (1336 shorter events, 139.6 us)
Async XLA Ops:
  7.2 1551.3 %all-gather.3.cloned.1.call-start = ((), (), s32[]{:S(2)}) async-start(), calls=%async_computation | async-start | bytes 50528256 | tf_op jit(solution)/shard_map/all_gather | solution.py:145
  7.3 5.3 copy-start.5
  10.2 631.7 %copy-start.3 = (f32[3,4,8,64]{3,2,1,0:T(8,128)}, f32[3,4,8,64]{3,2,1,0:T(8,128)S(1)}, u32[]{:S(2)}) copy-start(f32[3,4,8,64]{3,2,1,0:T(8,128)S(1)} %pad_maximum_fusion.20) | copy-start | bytes 73732
  642.8 146.7 %copy-start.8 = (f32[3,4,8,64]{3,2,1,0:T(8,128)S(1)}, f32[3,4,8,64]{3,2,1,0:T(8,128)}, u32[]{:S(2)}) copy-start(f32[3,4,8,64]{3,2,1,0:T(8,128)} %param.16) | copy-start | bytes 73732
  788.5 1.0 copy-start.1
  788.5 1.0 copy-start.2
  789.5 30.2 %copy-start = (f32[3,4,8,64]{3,2,1,0:T(8,128)}, f32[3,4,8,64]{3,2,1,0:T(8,128)S(1)}, u32[]{:S(2)}) copy-start(f32[3,4,8,64]{3,2,1,0:T(8,128)S(1)} %add.172) | copy-start | bytes 73732
  789.6 7.6 collective-permute-start
  789.7 7.8 collective-permute-start.1
  797.5 5.2 collective-permute-start.2
  797.6 5.1 collective-permute-start.3
  803.9 9.8 collective-permute-start.4
  804.0 9.8 collective-permute-start.5
  813.9 5.9 collective-permute-start.6
  814.0 5.8 collective-permute-start.7
  821.6 754.7 %copy-start.4 = (f32[6,512]{1,0:T(8,128)S(1)}, f32[6,512]{1,0:T(8,128)}, u32[]{:S(2)}) copy-start(f32[6,512]{1,0:T(8,128)} %param.12) | copy-start | bytes 36868
  821.6 754.7 %copy-start.6 = (f32[3,512]{1,0:T(4,128)S(1)}, f32[3,512]{1,0:T(4,128)}, u32[]{:S(2)}) copy-start(f32[3,512]{1,0:T(4,128)} %param.10) | copy-start | bytes 18436
  821.6 754.7 %copy-start.7 = (f32[3,512]{1,0:T(4,128)S(1)}, f32[3,512]{1,0:T(4,128)}, u32[]{:S(2)}) copy-start(f32[3,512]{1,0:T(4,128)} %param.11) | copy-start | bytes 18436
Sparse Core Ops, SparseCore 0:
  789.5 768.9 all-gather.2
